TPU v7x, 256 devices: a whole 4x4x8 slice. The times are simulated.
256 devices in a mesh: rows: 64 (over z, y, core), src: 4 (over x).
Axes of the slice: x: 4, y: 4, z: 8, core: 2. Of those that a mesh axis runs over, the one named last changes fastest.
Arguments:
- misfit: float32 [256, 64, 1024], P('rows', 'src'), may hold values from -6 to 6
- forward_fields: bfloat16 [256, 64, 1024], P('rows', 'src'), may hold values from -6 to 6
- contrast: float32 [256, 1024], P('rows'), may hold values from 0.2 to 0.6
- u_factors: bfloat16 [256, 16, 96, 1024], P('rows'), may hold values from -0.1875 to 0.1875
- v_factors: bfloat16 [256, 16, 96, 1024], P('rows'), may hold values from -0.1796875 to 0.1796875
- ranks: int32 [256, 16], P('rows'), may hold values from 32 to 96
- tile_cols: int32 [256, 16], replicated, may hold values from 0 to 255, as said below
- owner_slot: int32 [256], replicated, may hold values from 0 to 255, as said below
Outputs:
- adjoint_field: float32 [256, 64, 1024], P('rows', 'src')
- gradient: float32 [256, 1024], P('rows')
Inputs may be any that keep to these rules, and one draw needn't show every extreme that they name: The 16 entries of each row of tile_cols differ. With a tile's receiving device taken as owner_slot[tile_cols[s, k]] // 4 and its sending device as s // 4, at most 1 tiles of one sending device go to one receiving device, and every sending device sends exactly 1 to some receiving device. Each block of unknowns has exactly one slot: owner_slot is a permutation.
All inputs are finite; a program needn't handle non-finite values.
Results may differ from a plain program's by a relative error of at most 0.005.
Values may be sent and summed in bfloat16 or wider, within the bound.
A program may use at most 192 MiB of HBM per device.

v0:
```python
import jax
import jax.numpy as jnp
from jax import lax
from jax.sharding import PartitionSpec as P

B = 1024
K = 16
RMAX = 96
APPS = 4


def from_everyone(x, axis):
    count = lax.axis_size(axis)
    return lax.all_to_all(jnp.broadcast_to(x[None], (count, *x.shape)), axis, 0, 0, tiled=True)


def of_everyone(x, axis):
    return from_everyone(x, axis).sum(axis=0)


def route_tiles(tile_cols, owner_slot, rows_dev, peers):
    slot_count = owner_slot.shape[0]
    tiles = rows_dev * tile_cols.shape[1]
    match = (
        tile_cols.reshape(peers, tiles)[:, :, None]
        == jnp.arange(slot_count, dtype=jnp.int32)[None, None, :]
    )
    target_slot = jnp.sum(jnp.where(match, owner_slot[None, None, :], 0), axis=2)
    target_dev = target_slot // rows_dev
    local_slot = target_slot % rows_dev
    same = target_dev[:, :, None] == target_dev[:, None, :]
    before = jnp.arange(tiles)[None, :] < jnp.arange(tiles)[:, None]
    order = jnp.sum(jnp.where(same & before[None, :, :], 1, 0), axis=2).astype(jnp.int32)
    return (target_dev, local_slot, order)


def per_device(
    misfit, forward_fields, contrast, u_factors, v_factors, ranks, tile_cols, owner_slot
):
    rows_dev = u_factors.shape[0]
    tiles = rows_dev * K
    peers = lax.axis_size("rows")
    cap = (tiles + peers - 1) // peers
    sources = misfit.shape[1]
    here = lax.axis_index("rows")
    target_dev, local_slot, order = route_tiles(tile_cols, owner_slot, rows_dev, peers)
    mine_dev = lax.dynamic_index_in_dim(target_dev, here, 0, keepdims=False)
    mine_order = lax.dynamic_index_in_dim(order, here, 0, keepdims=False)
    box = mine_dev * cap + mine_order
    sender = jnp.arange(peers, dtype=jnp.int32)[:, None] * cap + order
    entry = jnp.where(target_dev == here, sender, peers * cap).reshape(-1)
    arrival = (
        jnp.full((peers * cap,), -1, jnp.int32).at[entry].set(local_slot.reshape(-1), mode="drop")
    )
    pick = (arrival[:, None] == jnp.arange(rows_dev, dtype=jnp.int32)[None, :]).astype(jnp.float32)
    keep = (jnp.arange(RMAX, dtype=jnp.int32)[None, None, :] < ranks[:, :, None]).astype(
        jnp.float32
    )
    field = misfit
    for step in range(APPS):
        coeff = jnp.einsum(
            "lsb,lkrb->lksr",
            field.astype(jnp.bfloat16),
            u_factors,
            preferred_element_type=jnp.float32,
        )
        tile_coeff = (coeff * keep[:, :, None, :]).astype(jnp.bfloat16)
        terms = jnp.einsum(
            "lksr,lkrb->lksb", tile_coeff, v_factors, preferred_element_type=jnp.float32
        )
        terms = terms.reshape(tiles, sources, B)
        outgoing = jnp.zeros((peers * cap, sources, B), jnp.float32).at[box].set(terms)
        incoming = lax.all_to_all(
            outgoing.reshape(peers, cap, sources, B).astype(jnp.bfloat16),
            "rows",
            split_axis=0,
            concat_axis=0,
            tiled=True,
        ).astype(jnp.float32)
        field = misfit + contrast[:, None, :] * jnp.einsum(
            "eq,esb->qsb",
            pick,
            incoming.reshape(peers * cap, sources, B),
            precision=lax.Precision.HIGHEST,
        )
    partial_sum = jnp.sum(forward_fields.astype(jnp.float32) * field, axis=1)
    total = of_everyone(partial_sum, "src")
    gradient = total * lax.rsqrt(jnp.float32(sources * lax.axis_size("src")))
    return (field, gradient)


def solution(mesh):
    placed = (
        P("rows", "src", None),
        P("rows", "src", None),
        P("rows", None),
        P("rows", None, None, None),
        P("rows", None, None, None),
        P("rows", None),
        P(),
        P(),
    )
    return jax.shard_map(
        per_device,
        mesh=mesh,
        in_specs=placed,
        out_specs=(P("rows", "src", None), P("rows", None)),
        check_vma=False,
    )
```

profile of v0, /device:TPU:1, one launch (start us, length us, event | category | flops | bytes accessed | tf_op | source)
XLA Modules:
  0.0 381.2 jit_solution(5792956069882785862)
XLA Ops:
  0.7 0.8 fusion.68
  1.4 0.8 copy.46
  2.2 0.1 eq.57
  2.3 2.5 select_reduce_fusion
  4.9 1.8 select_reduce_fusion.1
  6.8 8.5 %fusion.12 = bf16[4,16,96,16]{2,3,1,0:T(8,128)(2,1)S(1)} fusion(bf16[4,16,96,1024]{3,2,1,0:T(8,128)(2,1)} %param.11, f32[4,16,96]{2,1,0:T(8,128)S(1)} %fusion.68, f32[4,16,1024]{2,1,0:T(8,128)} %param.8), kind=kOutput, calls=%fused_computation.28 | convolution fusion | flops 201588736 | bytes 13066240 | tf_op jit(solution)/shard_map/lsb,lkrb->lksr/dot_general | solution.py:61
  15.2 8.3 %fusion.78 = f32[4,16,16,1024]{3,2,1,0:T(8,128)} fusion(bf16[4,16,96,16]{2,3,1,0:T(8,128)(2,1)S(1)} %fusion.12, bf16[4,16,96,1024]{3,2,1,0:T(8,128)(2,1)} %param.12), kind=kOutput, calls=%fused_computation.83 | convolution fusion | flops 201326592 | bytes 16973824 | tf_op jit(solution)/shard_map/lksr,lkrb->lksb/dot_general | solution.py:68
  23.6 2.5 broadcast.201.clone.2
  26.0 11.9 %scatter_fusion = f32[64,16,1024]{2,1,0:T(8,128)} fusion(f32[64,16,1024]{2,1,0:T(8,128)} %broadcast.201.clone.2, s32[64]{0:T(128)S(1)} %fusion.71, f32[64,16,1024]{2,1,0:T(8,128)} %bitcast.114), kind=kCustom, calls=%fused_computation.1 | custom fusion | bytes 12583168 | tf_op jit(solution)/shard_map/scatter | solution.py:72
  38.0 0.0 copy-start
  38.0 0.0 copy-start.1
  38.0 3.9 %convert_bitcast_fusion.3 = bf16[64,1,16,1024]{3,2,1,0:T(8,128)(2,1)} fusion(f32[64,16,1024]{2,1,0:T(8,128)} %scatter_fusion), kind=kLoop, calls=%fused_computation.22 | loop fusion | flops 1048576 | bytes 6291456 | tf_op jit(solution)/shard_map/convert_element_type | solution.py:74
  41.9 13.2 %all-to-all-start = ((bf16[64,1,16,1024]{3,2,1,0:T(8,128)(2,1)}), bf16[64,1,16,1024]{3,2,1,0:T(8,128)(2,1)S(1)}, u32[]{:S(2)}, u32[]{:S(2)}) async-start(bf16[64,1,16,1024]{3,2,1,0:T(8,128)(2,1)} %convert_bitcast_fusion.3), calls=%async_computation | async-start | bytes 4194304 | tf_op jit(solution)/shard_map/all_to_all | solution.py:73
  55.1 0.1 reduce_sum.43
  55.1 0.1 reduce_sum.41
  55.2 0.1 add.102
  55.4 0.1 compare_select_fusion
  55.5 15.7 %scatter_custom_fusion = s32[64]{0:T(128)S(1)} fusion(s32[4096]{0:T(1024)S(1)} %bitcast.117, s32[4096]{0:T(1024)S(1)} %add_select_fusion.1, s32[]{:T(128)} %constant.43.clone.1), kind=kCustom, calls=%fused_computation.81 | custom fusion | bytes 260 | tf_op jit(solution)/shard_map/scatter | solution.py:53
  71.1 33.6 %all-to-all-done = bf16[64,1,16,1024]{3,2,1,0:T(8,128)(2,1)S(1)} async-done(((bf16[64,1,16,1024]{3,2,1,0:T(8,128)(2,1)}), bf16[64,1,16,1024]{3,2,1,0:T(8,128)(2,1)S(1)}, u32[]{:S(2)}, u32[]{:S(2)}) %all-to-all-start) | async-done | bytes 2097184 | tf_op jit(solution)/shard_map/all_to_all | solution.py:73
  104.8 0.0 copy-done
  104.8 0.0 copy-done.1
  104.8 2.4 fusion.58
  107.2 6.9 %fusion.18 = bf16[4,16,16,96]{3,2,1,0:T(8,128)(2,1)S(1)} fusion(bf16[4,16,96,1024]{3,2,1,0:T(8,128)(2,1)} %param.11, f32[4,16,96]{2,1,0:T(8,128)S(1)} %fusion.68, bf16[4,16,1024,1]{2,0,1,3:T(4,128)(2,1)S(1)} %fusion.58), kind=kOutput, calls=%fused_computation.34 | convolution fusion | flops 201523200 | bytes 12935168 | tf_op jit(solution)/shard_map/lsb,lkrb->lksr/dot_general | solution.py:61
  114.1 8.3 %fusion.79 = f32[4,16,16,1024]{3,2,1,0:T(8,128)} fusion(bf16[4,16,16,96]{3,2,1,0:T(8,128)(2,1)S(1)} %fusion.18, bf16[4,16,96,1024]{3,2,1,0:T(8,128)(2,1)} %param.12), kind=kOutput, calls=%fused_computation.84 | convolution fusion | flops 201326592 | bytes 16973824 | tf_op jit(solution)/shard_map/lksr,lkrb->lksb/dot_general | solution.py:68
  122.4 2.5 broadcast.201.clone.1
  124.8 11.9 %scatter_fusion.1 = f32[64,16,1024]{2,1,0:T(8,128)} fusion(f32[64,16,1024]{2,1,0:T(8,128)} %broadcast.201.clone.1, s32[64]{0:T(128)S(1)} %fusion.71, f32[64,16,1024]{2,1,0:T(8,128)} %bitcast.115), kind=kCustom, calls=%fused_computation.2 | custom fusion | bytes 12583168 | tf_op jit(solution)/shard_map/scatter | solution.py:72
  136.8 2.5 convert_bitcast_fusion.2
  139.3 0.0 slice-start
  139.3 56.7 %all_to_all.25 = bf16[64,1,16,1024]{3,2,1,0:T(8,128)(2,1)S(1)} all-to-all(bf16[64,1,16,1024]{3,2,1,0:T(8,128)(2,1)S(1)} %convert_bitcast_fusion.2), channel_id=1, replica_groups=mesh['rows'=64,'src'=4] {'rows'}, dimensions={0} | all-to-all | bytes 4194304 | tf_op jit(solution)/shard_map/all_to_all | solution.py:73
  196.1 2.4 fusion.55
  198.5 0.0 slice-start.1
  198.5 0.0 slice-start.2
  198.5 7.1 %fusion.17 = bf16[4,16,16,96]{3,2,1,0:T(8,128)(2,1)S(1)} fusion(bf16[4,16,96,1024]{3,2,1,0:T(8,128)(2,1)} %param.11, f32[4,16,96]{2,1,0:T(8,128)S(1)} %fusion.68, bf16[4,16,1024,1]{2,0,1,3:T(4,128)(2,1)S(1)} %fusion.55), kind=kOutput, calls=%fused_computation.33 | convolution fusion | flops 201523200 | bytes 12935168 | tf_op jit(solution)/shard_map/lsb,lkrb->lksr/dot_general | solution.py:61
  205.5 0.0 slice-done
  205.5 0.0 slice-done.1
  205.6 0.0 slice-done.2
  205.6 3.3 fusion.80
  208.8 2.5 broadcast.201.clone
  211.3 11.9 %scatter_fusion.2 = f32[64,16,1024]{2,1,0:T(8,128)} fusion(f32[64,16,1024]{2,1,0:T(8,128)} %broadcast.201.clone, s32[64]{0:T(128)S(1)} %fusion.71, f32[64,16,1024]{2,1,0:T(8,128)} %bitcast.116), kind=kCustom, calls=%fused_computation.3 | custom fusion | bytes 12583168 | tf_op jit(solution)/shard_map/scatter | solution.py:72
  223.2 2.5 convert_bitcast_fusion.1
  225.7 0.0 slice-start.3
  225.7 56.7 %all_to_all.26 = bf16[64,1,16,1024]{3,2,1,0:T(8,128)(2,1)S(1)} all-to-all(bf16[64,1,16,1024]{3,2,1,0:T(8,128)(2,1)S(1)} %convert_bitcast_fusion.1), channel_id=1, replica_groups=mesh['rows'=64,'src'=4] {'rows'}, dimensions={0} | all-to-all | bytes 4194304 | tf_op jit(solution)/shard_map/all_to_all | solution.py:73
  282.5 2.4 fusion.52
  284.9 0.0 slice-start.4
  284.9 0.0 slice-start.5
  284.9 7.1 %fusion.16 = bf16[4,16,16,96]{3,2,1,0:T(8,128)(2,1)S(1)} fusion(bf16[4,16,96,1024]{3,2,1,0:T(8,128)(2,1)} %param.11, f32[4,16,96]{2,1,0:T(8,128)S(1)} %fusion.68, bf16[4,16,1024,1]{2,0,1,3:T(4,128)(2,1)S(1)} %fusion.52), kind=kOutput, calls=%fused_computation.32 | convolution fusion | flops 201523200 | bytes 12935168 | tf_op jit(solution)/shard_map/lsb,lkrb->lksr/dot_general | solution.py:61
  292.0 0.0 slice-done.3
  292.0 0.0 slice-done.4
  292.0 0.0 slice-done.5
  292.0 3.3 fusion.81
  295.2 2.5 broadcast.201
  297.7 11.9 %scatter_fusion.3 = f32[64,16,1024]{2,1,0:T(8,128)} fusion(f32[64,16,1024]{2,1,0:T(8,128)} %broadcast.201, s32[64]{0:T(128)S(1)} %fusion.71, f32[64,16,1024]{2,1,0:T(8,128)} %bitcast.113), kind=kCustom, calls=%fused_computation.4 | custom fusion | bytes 12583168 | tf_op jit(solution)/shard_map/scatter | solution.py:72
  309.6 0.0 copy-start.2
  309.6 2.5 convert_bitcast_fusion
  312.2 56.7 %all_to_all.27 = bf16[64,1,16,1024]{3,2,1,0:T(8,128)(2,1)S(1)} all-to-all(bf16[64,1,16,1024]{3,2,1,0:T(8,128)(2,1)S(1)} %convert_bitcast_fusion), channel_id=1, replica_groups=mesh['rows'=64,'src'=4] {'rows'}, dimensions={0} | all-to-all | bytes 4194304 | tf_op jit(solution)/shard_map/all_to_all | solution.py:73
  368.9 0.0 copy-done.2
  368.9 2.5 multiply_reduce_fusion
  371.4 0.6 broadcast_in_dim.34
  372.1 4.0 %all-to-all-start.4 = ((f32[4,4,1024]{2,1,0:T(4,128)}), f32[4,4,1024]{2,1,0:T(4,128)S(1)}, u32[]{:S(2)}, u32[]{:S(2)}) async-start(f32[4,4,1024]{2,1,0:T(4,128)} %broadcast_in_dim.34), calls=%async_computation.4 | async-start | bytes 131072 | tf_op jit(solution)/shard_map/all_to_all | solution.py:14
  376.1 0.9 copy.63
  376.9 3.6 all-to-all-done.4
  380.6 0.6 broadcast_multiply_fusion
  (8 shorter events, 0.1 us)
Async XLA Ops:
  38.0 66.8 %copy-start = (f32[4,16,1024]{2,1,0:T(8,128)S(1)}, f32[4,16,1024]{2,1,0:T(8,128)}, u32[]{:S(2)}) copy-start(f32[4,16,1024]{2,1,0:T(8,128)} %param.8) | copy-start | bytes 786436
  38.0 66.8 %copy-start.1 = (f32[4,1024]{1,0:T(4,128)S(1)}, f32[4,1024]{1,0:T(4,128)}, u32[]{:S(2)}) copy-start(f32[4,1024]{1,0:T(4,128)} %param.10) | copy-start | bytes 49156
  41.9 62.9 %all-to-all-start = ((bf16[64,1,16,1024]{3,2,1,0:T(8,128)(2,1)}), bf16[64,1,16,1024]{3,2,1,0:T(8,128)(2,1)S(1)}, u32[]{:S(2)}, u32[]{:S(2)}) async-start(bf16[64,1,16,1024]{3,2,1,0:T(8,128)(2,1)} %convert_bitcast_fusion.3), calls=%async_computation | async-start | bytes 4194304 | tf_op jit(solution)/shard_map/all_to_all | solution.py:73
  139.3 66.2 %slice-start = ((s8[12582912]{0:T(1024)(128)(4,1)}), s8[4194304]{0:T(1024)(128)(4,1)S(1)}, s32[]{:S(2)}) async-start(s8[12582912]{0:T(1024)(128)(4,1)} %bitcast.109), calls=%async_computation.5 | async-start | bytes 8388608
  198.5 7.1 %slice-start.1 = ((s8[12582912]{0:T(1024)(128)(4,1)}), s8[4194304]{0:T(1024)(128)(4,1)S(1)}, s32[]{:S(2)}) async-start(s8[12582912]{0:T(1024)(128)(4,1)} %bitcast.109), calls=%async_computation.6 | async-start | bytes 8388608
  198.5 7.1 %slice-start.2 = ((s8[12582912]{0:T(1024)(128)(4,1)}), s8[4194304]{0:T(1024)(128)(4,1)S(1)}, s32[]{:S(2)}) async-start(s8[12582912]{0:T(1024)(128)(4,1)} %bitcast.109), calls=%async_computation.7 | async-start | bytes 8388608
  225.7 66.2 %slice-start.3 = ((s8[12582912]{0:T(1024)(128)(4,1)}), s8[4194304]{0:T(1024)(128)(4,1)S(1)}, s32[]{:S(2)}) async-start(s8[12582912]{0:T(1024)(128)(4,1)} %bitcast.111), calls=%async_computation.8 | async-start | bytes 8388608
  284.9 7.1 %slice-start.4 = ((s8[12582912]{0:T(1024)(128)(4,1)}), s8[4194304]{0:T(1024)(128)(4,1)S(1)}, s32[]{:S(2)}) async-start(s8[12582912]{0:T(1024)(128)(4,1)} %bitcast.111), calls=%async_computation.9 | async-start | bytes 8388608
  284.9 7.1 %slice-start.5 = ((s8[12582912]{0:T(1024)(128)(4,1)}), s8[4194304]{0:T(1024)(128)(4,1)S(1)}, s32[]{:S(2)}) async-start(s8[12582912]{0:T(1024)(128)(4,1)} %bitcast.111), calls=%async_computation.10 | async-start | bytes 8388608
  309.6 59.3 %copy-start.2 = (bf16[4,16,1024]{2,1,0:T(8,128)(2,1)S(1)}, bf16[4,16,1024]{2,1,0:T(8,128)(2,1)}, u32[]{:S(2)}) copy-start(bf16[4,16,1024]{2,1,0:T(8,128)(2,1)} %param.9) | copy-start | bytes 393220
  372.1 8.5 %all-to-all-start.4 = ((f32[4,4,1024]{2,1,0:T(4,128)}), f32[4,4,1024]{2,1,0:T(4,128)S(1)}, u32[]{:S(2)}, u32[]{:S(2)}) async-start(f32[4,4,1024]{2,1,0:T(4,128)} %broadcast_in_dim.34), calls=%async_computation.4 | async-start | bytes 131072 | tf_op jit(solution)/shard_map/all_to_all | solution.py:14
where the time goes:
time: 384 us; the launch traced here: 381 us
  blocking collectives  170 us (44%)
  local copies, waits for them, and re-layouts  75.9 us (20%)
  matrix products  62.3 us (16%)
  waiting for transfers between devices  37.2 us (10%)
  other arithmetic  17.4 us (5%)
  starting transfers between devices  17.2 us (4%)
    all_to_all x3, blocking collectives, per_device(): lax.all_to_all(outgoing.reshape(peers, cap, sources, B).astype(jnp.bfloat...  170 us
    scatter x4, local copies, waits for them, and re-layouts, per_device(): jnp.zeros((peers * cap, sources, B), jnp.float32).at[box].set(terms)  47.8 us
    all_to_all x1, waiting for transfers between devices, per_device(): lax.all_to_all(outgoing.reshape(peers, cap, sources, B).astype(jnp.bfloat...  33.6 us
    dot_general x4, matrix products, per_device(): jnp.einsum('lsb,lkrb->lksr', field.astype(jnp.bfloat16), u_factors, prefe...  29.5 us
    dot_general x4, matrix products, per_device(): jnp.einsum('lksr,lkrb->lksb', tile_coeff, v_factors, preferred_element_ty...  23.1 us
    scatter x1, local copies, waits for them, and re-layouts, per_device(): jnp.full((peers * cap,), -1, jnp.int32).at[entry]  15.7 us
    all_to_all x1, starting transfers between devices, per_device(): lax.all_to_all(outgoing.reshape(peers, cap, sources, B).astype(jnp.bfloat...  13.2 us
    convert_element_type x4, other arithmetic, per_device(): outgoing.reshape(peers, cap, sources, B).astype(jnp.bfloat16)  11.4 us
  transfers between devices with their start and end apart: 2, of which 2 were waited for; matrix products, arithmetic and copies ran while one was open for 4% of the time, Pallas kernels for 0%

commit v1 on v0

v1 whole, which is shorter than its diff:
```python
import jax
import jax.numpy as jnp
from jax import lax
from jax.experimental import pallas as pl
from jax.experimental.pallas import tpu as pltpu
from jax.sharding import PartitionSpec as P

B = 1024
K = 16
RMAX = 96
APPS = 4
ROWS_DEV = 4
TILES = ROWS_DEV * K
NZ = 8
NY = 4
NM = 8
SRC = 16
PEERS = NZ * NM
NSRC = 4
MESH = pl.DeviceIdType.MESH
CONTRACT_LAST = (((1,), (1,)), ((), ()))
F32 = jnp.float32
BF16 = jnp.bfloat16
CHUNK = 256


def offset_of(k):
    return 4 + (1 - 2 * (k % 2)) * ((k + 1) // 2)


def kernel(
    tab,
    misfit,
    forward,
    contrast,
    onehot,
    u_hbm,
    v_hbm,
    field_ref,
    grad_ref,
    u,
    v,
    low,
    coeff,
    send,
    recv,
    zs,
    zin,
    gbuf,
    load_sem,
    send_sem,
    recv_sem,
    zs_sem,
    zr_sem,
    gs_sem,
    gr_sem,
):
    here = lax.axis_index("rows")
    me_src = lax.axis_index("src")
    z = here // NM
    m = here % NM
    y = m // 2
    c = m % 2

    load_u = pltpu.make_async_copy(u_hbm, u, load_sem.at[0])
    load_v = pltpu.make_async_copy(v_hbm, v, load_sem.at[1])
    load_u.start()
    load_v.start()

    z_up = {"rows": ((z + 1) % NZ) * NM + m}
    z_down = {"rows": ((z + NZ - 1) % NZ) * NM + m}
    peers = []
    for dy in (1, 3, 2, 0):
        for dc in (0, 1):
            if dy or dc:
                peers.append(((y + dy) % NY) * 2 + (c + dc) % 2)
    barrier = pltpu.get_barrier_semaphore()
    for mm in peers:
        pl.semaphore_signal(barrier, inc=1, device_id={"rows": z * NM + mm}, device_id_type=MESH)
    for dev in (z_up, z_down):
        pl.semaphore_signal(barrier, inc=1, device_id=dev, device_id_type=MESH)
    for ds in (1, 2, 3):
        pl.semaphore_signal(
            barrier, inc=1, device_id={"src": (me_src + ds) % NSRC}, device_id_type=MESH
        )

    for p in range(2):
        zin[p, 0] = jnp.zeros((TILES, B), BF16)
        zin[p, 1, 32:64] = jnp.zeros((32, B), BF16)
        zin[p, 2, 0:32] = jnp.zeros((32, B), BF16)
    low[...] = misfit[...].astype(BF16).reshape(ROWS_DEV, SRC, B)
    load_u.wait()
    load_v.wait()
    pl.semaphore_wait(barrier, len(peers) + 2 + NSRC - 1)

    order = peers + [m]
    lane = lax.broadcasted_iota(jnp.int32, (SRC, RMAX), 1)

    def y_copy(par, k, i):
        return pltpu.make_async_remote_copy(
            src_ref=send.at[k, i],
            dst_ref=recv.at[par, k, m],
            send_sem=send_sem.at[k, i],
            recv_sem=recv_sem.at[par, k, m],
            device_id={"rows": z * NM + order[i]},
            device_id_type=MESH,
        )

    def y_arrival(par, k, i):
        return pltpu.make_async_remote_copy(
            src_ref=send.at[k, i],
            dst_ref=recv.at[par, k, order[i]],
            send_sem=send_sem.at[k, i],
            recv_sem=recv_sem.at[par, k, order[i]],
            device_id={"rows": z * NM + order[i]},
            device_id_type=MESH,
        )

    def compute(par, k):
        zt = (z + offset_of(k)) % NZ
        for i in range(NM):
            d = zt * NM + order[i]
            j = tab[0, d]
            acc = lax.dot_general(low[tab[1, d]], u[j], CONTRACT_LAST, preferred_element_type=F32)
            coeff[i] = jnp.where(lane < tab[2, d], acc, 0.0).astype(BF16)
        for i in range(NM):
            d = zt * NM + order[i]
            terms = jnp.dot(coeff[i], v[tab[0, d]], preferred_element_type=F32).astype(BF16)
            if i < NM - 1:
                send[k, i] = terms
                y_copy(par, k, i).start()
            else:
                recv[par, k, m] = terms

    def z_full(par, k):
        return pltpu.make_async_remote_copy(
            src_ref=zs.at[k],
            dst_ref=zin.at[par, k + 2],
            send_sem=zs_sem.at[k],
            recv_sem=zr_sem.at[par, k + 2],
            device_id={"rows": ((z + NZ + 2 * (k % 2) - 1) % NZ) * NM + m},
            device_id_type=MESH,
        )

    def z_first(par, up):
        rows = pl.ds(0, 32) if up else pl.ds(32, 32)
        to = 1 if up else 2
        return pltpu.make_async_remote_copy(
            src_ref=zs.at[0, rows],
            dst_ref=zin.at[par, to, rows],
            send_sem=zs_sem.at[0 if up else 7],
            recv_sem=zr_sem.at[par, to],
            device_id=z_up if up else z_down,
            device_id_type=MESH,
        )

    def slot_sums(par, k, cols):
        got = recv[par, k, :, :, cols].reshape(NM * SRC, CHUNK)
        acc = jnp.dot(onehot[k], got, preferred_element_type=F32)
        return acc + zin[par, k, :, cols].astype(F32)

    def reduce(par, k):
        for i in range(NM - 1):
            y_arrival(par, k, i).wait_recv()

        @pl.when(k == 1)
        def _():
            z_first(par, True).wait_recv()

        @pl.when(k == 2)
        def _():
            z_first(par, False).wait_recv()

        @pl.when(k >= 3)
        def _():
            z_full(par, k - 2).wait_recv()

        @pl.when(k < 7)
        def _():
            for ch in range(B // CHUNK):
                cols = pl.ds(ch * CHUNK, CHUNK)
                zs[k, :, cols] = slot_sums(par, k, cols).astype(BF16)

        @pl.when(k == 0)
        def _():
            z_first(par, True).start()
            z_first(par, False).start()

        @pl.when((k > 0) & (k < 7))
        def _():
            z_full(par, k).start()

    def application(a, carry):
        par = a % 2

        def step(kk, inner):
            @pl.when(kk < NZ)
            def _():
                compute(par, kk)

            @pl.when((kk >= 2) & (kk < NZ + 1))
            def _():
                reduce(par, kk - 2)

            return inner

        lax.fori_loop(0, NZ + 1, step, 0)
        reduce(par, jnp.int32(7))
        z_full(par, 6).wait_recv()
        for ch in range(B // CHUNK):
            cols = pl.ds(ch * CHUNK, CHUNK)
            total = slot_sums(par, 7, cols) + zin[par, 8, :, cols].astype(F32)
            for s in range(ROWS_DEV):
                rows = pl.ds(s * SRC, SRC)
                value = (
                    misfit[rows, cols]
                    + contrast[pl.ds(s, 1), cols] * total[s * SRC : (s + 1) * SRC]
                )
                field_ref[rows, cols] = value
                low[s, :, cols] = value.astype(BF16)

        def drain(k, inner):
            for i in range(NM - 1):
                y_copy(par, k, i).wait_send()
            return inner

        lax.fori_loop(0, NZ, drain, 0)
        z_first(par, True).wait_send()
        z_first(par, False).wait_send()

        def z_drain(k, inner):
            z_full(par, k).wait_send()
            return inner

        lax.fori_loop(1, 7, z_drain, 0)
        return carry

    lax.fori_loop(0, APPS, application, 0)

    for s in range(ROWS_DEV):
        rows = pl.ds(s * SRC, SRC)
        product = forward[rows, :].astype(F32) * field_ref[rows, :]
        gbuf[0, pl.ds(s, 1), :] = jnp.sum(product, axis=0, keepdims=True)

    def g_copy(ds):
        return pltpu.make_async_remote_copy(
            src_ref=gbuf.at[0],
            dst_ref=gbuf.at[ds],
            send_sem=gs_sem.at[ds],
            recv_sem=gr_sem.at[ds],
            device_id={"src": (me_src + ds) % NSRC},
            device_id_type=MESH,
        )

    for ds in (1, 2, 3):
        g_copy(ds).start()
    for ds in (1, 2, 3):
        g_copy(ds).wait()
    even = (gbuf[0] + gbuf[2], gbuf[1] + gbuf[3])
    grad_ref[...] = (even[0] + even[1]) * (NSRC * SRC) ** -0.5


def tables(ranks, tile_cols, owner_slot):
    here = lax.axis_index("rows")
    z, m = here // NM, here % NM
    plane = lax.dynamic_slice_in_dim(tile_cols.reshape(NZ, NM, TILES), z, 1, 0)[0]
    slots = jnp.arange(owner_slot.shape[0], dtype=jnp.int32)
    target = jnp.sum(jnp.where(plane[:, :, None] == slots, owner_slot, 0), axis=2)
    target_dev, local = target // ROWS_DEV, target % ROWS_DEV
    mine = lax.dynamic_index_in_dim(target_dev, m, 0, keepdims=False)
    goes = mine[None, :] == jnp.arange(PEERS, dtype=jnp.int32)[:, None]
    tiles = jnp.arange(TILES, dtype=jnp.int32)
    values = jnp.stack([tiles, tiles // K, ranks.reshape(TILES)])
    tab = jnp.sum(jnp.where(goes[None], values[:, None, :], 0), axis=2)
    ks = jnp.arange(NZ, dtype=jnp.int32)
    dest = ((z + offset_of(ks)) % NZ) * NM + m
    comes = target_dev[None] == dest[:, None, None]
    q = jnp.sum(jnp.where(comes, local[None], 0), axis=2)
    row = jnp.arange(TILES, dtype=jnp.int32)[:, None]
    col = jnp.arange(NM * SRC, dtype=jnp.int32)[None, :]
    same = (row % SRC) == (col % SRC)
    onehot = (jnp.repeat(q, SRC, axis=1)[:, None, :] == (row // SRC)[None]) & same[None]
    return tab.astype(jnp.int32), onehot.astype(BF16)


def per_device(
    misfit, forward_fields, contrast, u_factors, v_factors, ranks, tile_cols, owner_slot
):
    tab, onehot = tables(ranks, tile_cols, owner_slot)
    vmem = pl.BlockSpec(memory_space=pltpu.VMEM)
    hbm = pl.BlockSpec(memory_space=pl.ANY)
    dma = pltpu.SemaphoreType.DMA
    field, gradient = pl.pallas_call(
        kernel,
        out_shape=(
            jax.ShapeDtypeStruct((TILES, B), F32),
            jax.ShapeDtypeStruct((ROWS_DEV, B), F32),
        ),
        in_specs=[pl.BlockSpec(memory_space=pltpu.SMEM), vmem, vmem, vmem, vmem, hbm, hbm],
        out_specs=(vmem, vmem),
        scratch_shapes=[
            pltpu.VMEM((TILES, RMAX, B), BF16),
            pltpu.VMEM((TILES, RMAX, B), BF16),
            pltpu.VMEM((ROWS_DEV, SRC, B), BF16),
            pltpu.VMEM((NM, SRC, RMAX), BF16),
            pltpu.VMEM((NZ, NM - 1, SRC, B), BF16),
            pltpu.VMEM((2, NZ, NM, SRC, B), BF16),
            pltpu.VMEM((7, TILES, B), BF16),
            pltpu.VMEM((2, 9, TILES, B), BF16),
            pltpu.VMEM((NSRC, ROWS_DEV, B), F32),
            dma((2,)),
            dma((NZ, NM - 1)),
            dma((2, NZ, NM)),
            dma((8,)),
            dma((2, 9)),
            dma((NSRC,)),
            dma((NSRC,)),
        ],
        compiler_params=pltpu.CompilerParams(
            collective_id=0, has_side_effects=True, vmem_limit_bytes=58 * 1024 * 1024
        ),
    )(
        tab,
        misfit.reshape(TILES, B),
        forward_fields.reshape(TILES, B),
        contrast,
        onehot,
        u_factors.reshape(TILES, RMAX, B),
        v_factors.reshape(TILES, RMAX, B),
    )
    return field.reshape(ROWS_DEV, SRC, B), gradient


def solution(mesh):
    placed = (
        P("rows", "src", None),
        P("rows", "src", None),
        P("rows", None),
        P("rows", None, None, None),
        P("rows", None, None, None),
        P("rows", None),
        P(),
        P(),
    )
    return jax.shard_map(
        per_device,
        mesh=mesh,
        in_specs=placed,
        out_specs=(P("rows", "src", None), P("rows", None)),
        check_vma=False,
    )
```

time: 384 us -> 147 us (0.38)
  blocking collectives: 170 us -> 0 us
  Pallas kernels: 0 us -> 138 us
  local copies, waits for them, and re-layouts: 75.9 us -> 4.84 us
  matrix products: 62.3 us -> 0 us
  waiting for transfers between devices: 37.2 us -> 0 us
  starting transfers between devices: 17.2 us -> 0 us
  other arithmetic: 17.4 us -> 2.93 us
    all_to_all x3 -> x0, blocking collectives: 170 us -> none  [per_device(): lax.all_to_all(outgoing.reshape(peers, cap, sources, B).astype(jnp.bfloat...]
    pallas_call x0 -> x1, Pallas kernels: none -> 138 us  [per_device(): pl.pallas_call(kernel, out_shape=(jax.ShapeDtypeStruct((TILES, B), F32),...]
    scatter x5 -> x0, local copies, waits for them, and re-layouts: 63.4 us -> none  [the longest x4 47.8 us: per_device(): jnp.zeros((peers * cap, sources, B), jnp.float32).at[box].set(terms)]
    dot_general x12 -> x0, matrix products: 62.3 us -> none  [the longest x4 29.5 us: per_device(): jnp.einsum('lsb,lkrb->lksr', field.astype(jnp.bfloat16), u_factors, prefe...]
    all_to_all x2 -> x0, waiting for transfers between devices: 37.2 us -> none  [the longest x1 33.6 us: per_device(): lax.all_to_all(outgoing.reshape(peers, cap, sources, B).astype(jnp.bfloat...]
    all_to_all x2 -> x0, starting transfers between devices: 17.2 us -> none  [the longest x1 13.2 us: per_device(): lax.all_to_all(outgoing.reshape(peers, cap, sources, B).astype(jnp.bfloat...]
    convert_element_type x5 -> x1, other arithmetic: 12.2 us -> 0.78 us  [tables(): return (tab.astype(jnp.int32), onehot.astype(BF16))]
    another operation x4 -> x1, local copies, waits for them, and re-layouts: 9.81 us -> 0.77 us  [tables(): values = jnp.stack([tiles, tiles // K, ranks.reshape(TILES)])]
  transfers between devices with their start and end apart: 2 -> 0, of which waited for: 2 -> 0; matrix products, arithmetic and copies ran while one was open for 4% -> 0% of each run, Pallas kernels for 0% -> 0%
where the time goes in v1:
time: 147 us; the launch traced here: 146 us
  Pallas kernels  138 us (94%)
  local copies, waits for them, and re-layouts  4.84 us (3%)
  other arithmetic  2.93 us (2%)
    pallas_call x1, Pallas kernels, per_device(): pl.pallas_call(kernel, out_shape=(jax.ShapeDtypeStruct((TILES, B), F32),...  138 us
    unnamed x3, local copies, waits for them, and re-layouts  3.81 us

profile of v1, /device:TPU:1, one launch (start us, length us, event | category | flops | bytes accessed | tf_op | source)
XLA Modules:
  0.0 146.3 jit_solution(8575208212593950106)
XLA Ops:
  0.7 0.8 stack_reshape.3
  1.5 0.1 broadcast_compare_fusion
  1.6 0.8 copy.11
  2.4 0.1 reshape.250
  2.5 1.0 select_reduce_fusion
  3.5 0.3 select_reduce_fusion.2
  3.8 0.7 select_reduce_fusion.1.tab
  4.6 0.1 broadcast_in_dim.62
  4.6 0.1 eq.98
  4.7 0.8 and_convert_fusion.onehot
  5.5 137.8 %shard_map.95 = (f32[64,1024]{1,0:T(8,128)}, f32[4,1024]{1,0:T(4,128)}) custom-call(s32[3,64]{1,0:T(4,128)} %select_reduce_fusion.1.tab, f32[64,1024]{1,0:T(8,128)} %bitcast.11, bf16[64,1024]{1,0:T(8,128)(2,1)} %bitcast.13, f32[4,1024]{1,0:T(4,128)} %contrast.1, bf16[8,64,128]{2,1,0:T(8,128)(2,1)} %and_convert_fusion.onehot, bf16[64,96,1024]{2,1,0:T(8,128)(2,1)} %bitcast.9, ...), custom_call_target="tpu_custom_call" | custom-call | tf_op jit(solution)/shard_map/pallas_call | solution.py:293
  143.3 1.7 %copy.14 = f32[4,16,1024]{2,1,0:T(8,128)} copy(f32[4,16,1024]{2,1,0:T(8,128)} %bitcast.12) | data formatting | bytes 524288
  145.0 1.3 copy.15
  (10 shorter events, 0.1 us)

commit v2 on v1

v2 whole, which is shorter than its diff:
```python
import jax
import jax.numpy as jnp
from jax import lax
from jax.experimental import pallas as pl
from jax.experimental.pallas import tpu as pltpu
from jax.sharding import PartitionSpec as P

B = 1024
K = 16
RMAX = 96
APPS = 4
ROWS_DEV = 4
TILES = ROWS_DEV * K
NZ = 8
NY = 4
NM = 8
SRC = 16
PEERS = NZ * NM
NSRC = 4
MESH = pl.DeviceIdType.MESH
CONTRACT_LAST = (((1,), (1,)), ((), ()))
F32 = jnp.float32
BF16 = jnp.bfloat16
CHUNK = 256
HALF = 8
LAG = 2


def offsets_of(p):
    far = 4 - 2 * p + 3 * (p // 2)
    return far, jnp.minimum(p, 1) * (NZ - far)


def kernel(
    tab,
    misfit,
    forward,
    contrast,
    onehot,
    u_hbm,
    v_hbm,
    field_ref,
    grad_ref,
    u,
    v,
    low,
    coeff,
    send,
    recv,
    zs,
    zin,
    own,
    gbuf,
    load_sem,
    send_sem,
    recv_sem,
    zs_sem,
    zr_sem,
    gs_sem,
    gr_sem,
):
    here = lax.axis_index("rows")
    me_src = lax.axis_index("src")
    z = here // NM
    m = here % NM
    y = m // 2
    c = m % 2

    load_u = pltpu.make_async_copy(u_hbm, u, load_sem.at[0])
    load_v = pltpu.make_async_copy(v_hbm, v, load_sem.at[1])
    load_u.start()
    load_v.start()

    def z_dev(dz):
        return {"rows": ((z + NZ + dz) % NZ) * NM + m}

    peers = []
    for dy in (2, 1, 3, 0):
        for dc in (0, 1):
            if dy or dc:
                peers.append(((y + dy) % NY) * 2 + (c + dc) % 2)
    barrier = pltpu.get_barrier_semaphore()
    for mm in peers:
        pl.semaphore_signal(barrier, inc=1, device_id={"rows": z * NM + mm}, device_id_type=MESH)
    for dz in (1, -1, 3, -3):
        pl.semaphore_signal(barrier, inc=1, device_id=z_dev(dz), device_id_type=MESH)
    for ds in (1, 2, 3):
        pl.semaphore_signal(
            barrier, inc=1, device_id={"src": (me_src + ds) % NSRC}, device_id_type=MESH
        )

    for b in range(4):
        zin[b, 0, 16:48] = jnp.zeros((32, B), BF16)
    for h in range(2):
        for s in range(ROWS_DEV):
            low[h, s] = misfit[pl.ds(s * SRC + h * HALF, HALF), :].astype(BF16)
    load_u.wait()
    load_v.wait()
    pl.semaphore_wait(barrier, len(peers) + 4 + NSRC - 1)

    order = peers + [m]
    lane = lax.broadcasted_iota(jnp.int32, (HALF, RMAX), 1)

    def y_copy(ph, p, i):
        return pltpu.make_async_remote_copy(
            src_ref=send.at[ph % 2, p, i],
            dst_ref=recv.at[ph % 4, p, m],
            send_sem=send_sem.at[ph % 2, p, i],
            recv_sem=recv_sem.at[ph % 4, p, m],
            device_id={"rows": z * NM + order[i]},
            device_id_type=MESH,
        )

    def y_arrival(ph, p, i):
        return pltpu.make_async_remote_copy(
            src_ref=send.at[ph % 2, p, i],
            dst_ref=recv.at[ph % 4, p, order[i]],
            send_sem=send_sem.at[ph % 2, p, i],
            recv_sem=recv_sem.at[ph % 4, p, order[i]],
            device_id={"rows": z * NM + order[i]},
            device_id_type=MESH,
        )

    def compute(ph, p):
        h = ph % 2

        @pl.when(ph >= 2)
        def _():
            for i in range(NM - 1):
                y_copy(ph, p, i).wait_send()

        layers = [(z + off) % NZ for off in offsets_of(p)]
        for i in range(NM):
            for q in range(2):
                d = layers[q] * NM + order[i]
                j = tab[0, d]
                acc = lax.dot_general(
                    low[h, tab[1, d]], u[j], CONTRACT_LAST, preferred_element_type=F32
                )
                coeff[i, q] = jnp.where(lane < tab[2, d], acc, 0.0)
        for i in range(NM):
            terms = []
            for q in range(2):
                d = layers[q] * NM + order[i]
                terms.append(
                    jnp.dot(
                        coeff[i, q].astype(BF16), v[tab[0, d]], preferred_element_type=F32
                    )
                )
            block = jnp.concatenate(terms, axis=0).astype(BF16)
            if i < NM - 1:
                send[h, p, i] = block
                y_copy(ph, p, i).start()
            else:
                recv[ph % 4, p, m] = block

    def z_full(ph, p, way):
        rows = pl.ds(way * 32, 32)
        return pltpu.make_async_remote_copy(
            src_ref=zs.at[ph % 2, p, rows],
            dst_ref=zin.at[ph % 4, p, rows],
            send_sem=zs_sem.at[ph % 2, p, way],
            recv_sem=zr_sem.at[ph % 4, p, way],
            device_id=z_dev((1 - 2 * way) * (3 - 2 * (p % 2))),
            device_id_type=MESH,
        )

    def z_first(ph, way):
        return pltpu.make_async_remote_copy(
            src_ref=zs.at[ph % 2, 0, pl.ds(way * 16, 16)],
            dst_ref=zin.at[ph % 4, 0, pl.ds(way * 48, 16)],
            send_sem=zs_sem.at[ph % 2, 0, way],
            recv_sem=zr_sem.at[ph % 4, 0, way],
            device_id=z_dev(1 - 2 * way),
            device_id_type=MESH,
        )

    def reduce(ph, p):
        h = ph % 2
        for i in range(NM - 1):
            y_arrival(ph, p, i).wait_recv()

        def y_sums(cols):
            got = recv[ph % 4, p, :, :, cols].reshape(NM * SRC, CHUNK)
            return jnp.dot(onehot[p], got, preferred_element_type=F32)

        @pl.when(p == 0)
        def _():
            @pl.when(ph >= 2)
            def _():
                for way in range(2):
                    z_first(ph, way).wait_send()

            for ch in range(B // CHUNK):
                cols = pl.ds(ch * CHUNK, CHUNK)
                acc = y_sums(cols)
                zs[h, 0, 0:32, cols] = acc[0:32].astype(BF16)
                own[h, :, cols] = acc[32:64]
            for way in range(2):
                z_first(ph, way).start()

        @pl.when(p > 0)
        def _():
            @pl.when(ph >= 2)
            def _():
                for way in range(2):
                    z_full(ph, p, way).wait_send()

            @pl.when(p == 2)
            def _():
                for way in range(2):
                    z_first(ph, way).wait_recv()

            @pl.when(p == 3)
            def _():
                for way in range(2):
                    z_full(ph, 1, way).wait_recv()

            @pl.when(p == 1)
            def _():
                for ch in range(B // CHUNK):
                    cols = pl.ds(ch * CHUNK, CHUNK)
                    zs[h, p, :, cols] = y_sums(cols).astype(BF16)

            @pl.when(p > 1)
            def _():
                for ch in range(B // CHUNK):
                    cols = pl.ds(ch * CHUNK, CHUNK)
                    acc = y_sums(cols) + zin[ph % 4, p - 2, :, cols].astype(F32)
                    zs[h, p, :, cols] = acc.astype(BF16)

            for way in range(2):
                z_full(ph, p, way).start()

    def finish(ph):
        h = ph % 2
        for p in (2, 3):
            for way in range(2):
                z_full(ph, p, way).wait_recv()
        for ch in range(B // CHUNK):
            cols = pl.ds(ch * CHUNK, CHUNK)
            arrived = zin[ph % 4, 2, :, cols].astype(F32) + zin[ph % 4, 3, :, cols].astype(F32)
            total = own[h, :, cols] + arrived[0:32] + arrived[32:64]
            for s in range(ROWS_DEV):
                rows = pl.ds(pl.multiple_of(s * SRC + h * HALF, HALF), HALF)
                value = (
                    misfit[rows, cols]
                    + contrast[pl.ds(s, 1), cols] * total[s * HALF : (s + 1) * HALF]
                )
                field_ref[rows, cols] = value
                low[h, s, :, cols] = value.astype(BF16)

    steps = 2 * APPS * 4

    def step(g, carry):
        @pl.when(g < steps)
        def _():
            compute(g // 4, g % 4)

        @pl.when(g >= LAG)
        def _():
            back = g - LAG
            reduce(back // 4, back % 4)

        @pl.when((g % 4 == 3) & (g >= 7))
        def _():
            finish(g // 4 - 1)

        return carry

    lax.fori_loop(0, steps + LAG, step, 0)
    finish(2 * APPS - 1)

    for ph in (2 * APPS - 2, 2 * APPS - 1):
        for p in range(4):
            for i in range(NM - 1):
                y_copy(ph, p, i).wait_send()
            for way in range(2):
                (z_full(ph, p, way) if p else z_first(ph, way)).wait_send()

    for s in range(ROWS_DEV):
        rows = pl.ds(s * SRC, SRC)
        product = forward[rows, :].astype(F32) * field_ref[rows, :]
        gbuf[0, pl.ds(s, 1), :] = jnp.sum(product, axis=0, keepdims=True)

    def g_copy(ds):
        return pltpu.make_async_remote_copy(
            src_ref=gbuf.at[0],
            dst_ref=gbuf.at[ds],
            send_sem=gs_sem.at[ds],
            recv_sem=gr_sem.at[ds],
            device_id={"src": (me_src + ds) % NSRC},
            device_id_type=MESH,
        )

    for ds in (1, 2, 3):
        g_copy(ds).start()
    for ds in (1, 2, 3):
        g_copy(ds).wait()
    even = (gbuf[0] + gbuf[2], gbuf[1] + gbuf[3])
    grad_ref[...] = (even[0] + even[1]) * (NSRC * SRC) ** -0.5


def tables(ranks, tile_cols, owner_slot):
    here = lax.axis_index("rows")
    z, m = here // NM, here % NM
    plane = lax.dynamic_slice_in_dim(tile_cols.reshape(NZ, NM, TILES), z, 1, 0)[0]
    slots = jnp.arange(owner_slot.shape[0], dtype=jnp.int32)
    target = jnp.sum(jnp.where(plane[:, :, None] == slots, owner_slot, 0), axis=2)
    target_dev, local = target // ROWS_DEV, target % ROWS_DEV
    mine = lax.dynamic_index_in_dim(target_dev, m, 0, keepdims=False)
    goes = mine[None, :] == jnp.arange(PEERS, dtype=jnp.int32)[:, None]
    tiles = jnp.arange(TILES, dtype=jnp.int32)
    values = jnp.stack([tiles, tiles // K, ranks.reshape(TILES)])
    tab = jnp.sum(jnp.where(goes[None], values[:, None, :], 0), axis=2)
    layer = jnp.concatenate([z + off for off in offsets_of(jnp.arange(4, dtype=jnp.int32))])
    dest = (layer % NZ) * NM + m
    comes = target_dev[None] == dest[:, None, None]
    q = jnp.sum(jnp.where(comes, local[None], 0), axis=2).reshape(2, 4, NM)
    row = jnp.arange(TILES, dtype=jnp.int32)[:, None]
    col = jnp.arange(NM * SRC, dtype=jnp.int32)[None, :]
    same = ((row % HALF) == (col % HALF)) & ((row // 32) == (col // HALF % 2))
    slot = jnp.repeat(q, SRC, axis=2)
    slot = jnp.where((row // 32)[None] == 0, slot[0][:, None, :], slot[1][:, None, :])
    onehot = (slot == (row // HALF % ROWS_DEV)[None]) & same[None]
    return tab.astype(jnp.int32), onehot.astype(BF16)


def per_device(
    misfit, forward_fields, contrast, u_factors, v_factors, ranks, tile_cols, owner_slot
):
    tab, onehot = tables(ranks, tile_cols, owner_slot)
    vmem = pl.BlockSpec(memory_space=pltpu.VMEM)
    hbm = pl.BlockSpec(memory_space=pl.ANY)
    dma = pltpu.SemaphoreType.DMA
    field, gradient = pl.pallas_call(
        kernel,
        out_shape=(
            jax.ShapeDtypeStruct((TILES, B), F32),
            jax.ShapeDtypeStruct((ROWS_DEV, B), F32),
        ),
        in_specs=[pl.BlockSpec(memory_space=pltpu.SMEM), vmem, vmem, vmem, vmem, hbm, hbm],
        out_specs=(vmem, vmem),
        scratch_shapes=[
            pltpu.VMEM((TILES, RMAX, B), BF16),
            pltpu.VMEM((TILES, RMAX, B), BF16),
            pltpu.VMEM((2, ROWS_DEV, HALF, B), BF16),
            pltpu.VMEM((NM, 2, HALF, RMAX), F32),
            pltpu.VMEM((2, 4, NM - 1, SRC, B), BF16),
            pltpu.VMEM((4, 4, NM, SRC, B), BF16),
            pltpu.VMEM((2, 4, TILES, B), BF16),
            pltpu.VMEM((4, 4, TILES, B), BF16),
            pltpu.VMEM((2, 32, B), F32),
            pltpu.VMEM((NSRC, ROWS_DEV, B), F32),
            dma((2,)),
            dma((2, 4, NM - 1)),
            dma((4, 4, NM)),
            dma((2, 4, 2)),
            dma((4, 4, 2)),
            dma((NSRC,)),
            dma((NSRC,)),
        ],
        compiler_params=pltpu.CompilerParams(
            collective_id=0, has_side_effects=True, vmem_limit_bytes=58 * 1024 * 1024
        ),
    )(
        tab,
        misfit.reshape(TILES, B),
        forward_fields.reshape(TILES, B),
        contrast,
        onehot,
        u_factors.reshape(TILES, RMAX, B),
        v_factors.reshape(TILES, RMAX, B),
    )
    return field.reshape(ROWS_DEV, SRC, B), gradient


def solution(mesh):
    placed = (
        P("rows", "src", None),
        P("rows", "src", None),
        P("rows", None),
        P("rows", None, None, None),
        P("rows", None, None, None),
        P("rows", None),
        P(),
        P(),
    )
    return jax.shard_map(
        per_device,
        mesh=mesh,
        in_specs=placed,
        out_specs=(P("rows", "src", None), P("rows", None)),
        check_vma=False,
    )
```

time: 147 us -> 132 us (0.90)
  Pallas kernels: 138 us -> 123 us
    pallas_call x1, Pallas kernels: 138 us -> 123 us  [per_device(): pl.pallas_call(kernel, out_shape=(jax.ShapeDtypeStruct((TILES, B), F32),...]
where the time goes in v2:
time: 132 us; the launch traced here: 131 us
  Pallas kernels  123 us (93%)
  local copies, waits for them, and re-layouts  4.99 us (4%)
  other arithmetic  2.99 us (2%)
    pallas_call x1, Pallas kernels, per_device(): pl.pallas_call(kernel, out_shape=(jax.ShapeDtypeStruct((TILES, B), F32),...  123 us
    unnamed x3, local copies, waits for them, and re-layouts  3.81 us

profile of v2, /device:TPU:1, one launch (start us, length us, event | category | flops | bytes accessed | tf_op | source)
XLA Modules:
  0.0 131.4 jit_solution(14545990155429984081)
XLA Ops:
  0.7 0.8 stack_reshape.3
  1.5 0.1 fusion.8
  1.6 0.1 compare_and_fusion
  1.7 0.8 copy.11
  2.5 0.1 reshape.407
  2.6 1.0 select_reduce_fusion
  3.6 0.3 select_reduce_fusion.2
  4.0 0.7 select_reduce_fusion.1.tab
  4.7 0.1 broadcast_in_dim.94
  4.8 0.1 broadcast_in_dim.95
  4.8 0.1 broadcast_in_dim.97
  4.9 0.1 broadcast_in_dim.98
  5.0 0.7 fusion.1.onehot
  5.7 122.7 %shard_map.95 = (f32[64,1024]{1,0:T(8,128)}, f32[4,1024]{1,0:T(4,128)}) custom-call(s32[3,64]{1,0:T(4,128)} %select_reduce_fusion.1.tab, f32[64,1024]{1,0:T(8,128)} %bitcast.11, bf16[64,1024]{1,0:T(8,128)(2,1)} %bitcast.13, f32[4,1024]{1,0:T(4,128)} %contrast.1, bf16[4,64,128]{2,1,0:T(8,128)(2,1)} %fusion.1.onehot, bf16[64,96,1024]{2,1,0:T(8,128)(2,1)} %bitcast.9, ...), custom_call_target="tpu_custom_call" | custom-call | tf_op jit(solution)/shard_map/pallas_call | solution.py:336
  128.4 1.7 %copy.14 = f32[4,16,1024]{2,1,0:T(8,128)} copy(f32[4,16,1024]{2,1,0:T(8,128)} %bitcast.12) | data formatting | bytes 524288
  130.1 1.3 %copy.15 = f32[4,1024]{1,0:T(4,128)} copy(f32[4,1024]{1,0:T(4,128)} %get-tuple-element.19) | data formatting | bytes 32768
  (13 shorter events, 0.1 us)

commit v3 on v2

--- a/solution.py
+++ b/solution.py
@@ -24,6 +24,7 @@
 CHUNK = 256
 HALF = 8
 LAG = 2
+CODE = 128
 
 
 def offsets_of(p):
@@ -36,7 +37,7 @@
     misfit,
     forward,
     contrast,
-    onehot,
+    slot_of,
     u_hbm,
     v_hbm,
     field_ref,
@@ -50,6 +51,7 @@
     zs,
     zin,
     own,
+    onehot,
     gbuf,
     load_sem,
     send_sem,
@@ -66,10 +68,13 @@
     y = m // 2
     c = m % 2
 
-    load_u = pltpu.make_async_copy(u_hbm, u, load_sem.at[0])
-    load_v = pltpu.make_async_copy(v_hbm, v, load_sem.at[1])
-    load_u.start()
-    load_v.start()
+    def load(n):
+        tiles = pl.ds(n % 2 * (TILES // 2), TILES // 2)
+        src, dst = ((u_hbm, u), (v_hbm, v))[n // 2]
+        return pltpu.make_async_copy(src.at[tiles], dst.at[tiles], load_sem.at[n])
+
+    load(0).start()
+    load(1).start()
 
     def z_dev(dz):
         return {"rows": ((z + NZ + dz) % NZ) * NM + m}
@@ -94,9 +99,21 @@
     for h in range(2):
         for s in range(ROWS_DEV):
             low[h, s] = misfit[pl.ds(s * SRC + h * HALF, HALF), :].astype(BF16)
-    load_u.wait()
-    load_v.wait()
-    pl.semaphore_wait(barrier, len(peers) + 4 + NSRC - 1)
+    row = lax.broadcasted_iota(jnp.int32, (TILES, NM * SRC), 0)
+    col = lax.broadcasted_iota(jnp.int32, (TILES, NM * SRC), 1)
+    same = ((row % HALF) == (col % HALF)) & ((row // 32) == (col // HALF % 2))
+    for p in range(4):
+        slot = jnp.zeros((TILES, NM * SRC), jnp.int32)
+        for half in range(2):
+            for mm in range(NM):
+                where = (col // SRC == mm) & (row // 32 == half)
+                slot = jnp.where(where, slot_of[half * 32 + p * NM + mm], slot)
+        hit = same & (slot == row // HALF % ROWS_DEV)
+        onehot[p] = jnp.where(hit, 1.0, 0.0).astype(BF16)
+    load(0).wait()
+    load(2).start()
+    load(1).wait()
+    load(3).start()
 
     order = peers + [m]
     lane = lax.broadcasted_iota(jnp.int32, (HALF, RMAX), 1)
@@ -121,30 +138,32 @@
             device_id_type=MESH,
         )
 
-    def compute(ph, p):
+    def layers_of(p):
+        return [(z + off) % NZ for off in offsets_of(p)]
+
+    def coefficients(ph, p):
         h = ph % 2
-
-        @pl.when(ph >= 2)
-        def _():
-            for i in range(NM - 1):
-                y_copy(ph, p, i).wait_send()
-
-        layers = [(z + off) % NZ for off in offsets_of(p)]
+        layers = layers_of(p)
         for i in range(NM):
             for q in range(2):
                 d = layers[q] * NM + order[i]
-                j = tab[0, d]
+                code = tab[d]
+                j = code // CODE
                 acc = lax.dot_general(
-                    low[h, tab[1, d]], u[j], CONTRACT_LAST, preferred_element_type=F32
+                    low[h, code // (CODE * K)], u[j], CONTRACT_LAST, preferred_element_type=F32
                 )
-                coeff[i, q] = jnp.where(lane < tab[2, d], acc, 0.0)
+                coeff[i, q] = jnp.where(lane < code % CODE, acc, 0.0)
+
+    def send_terms(ph, p):
+        h = ph % 2
+        layers = layers_of(p)
         for i in range(NM):
             terms = []
             for q in range(2):
                 d = layers[q] * NM + order[i]
                 terms.append(
                     jnp.dot(
-                        coeff[i, q].astype(BF16), v[tab[0, d]], preferred_element_type=F32
+                        coeff[i, q].astype(BF16), v[tab[d] // CODE], preferred_element_type=F32
                     )
                 )
             block = jnp.concatenate(terms, axis=0).astype(BF16)
@@ -255,7 +274,15 @@
     def step(g, carry):
         @pl.when(g < steps)
         def _():
-            compute(g // 4, g % 4)
+            ph, p = g // 4, g % 4
+
+            @pl.when(ph >= 2)
+            def _():
+                for i in range(NM - 1):
+                    y_copy(ph, p, i).wait_send()
+
+            coefficients(ph, p)
+            send_terms(ph, p)
 
         @pl.when(g >= LAG)
         def _():
@@ -268,7 +295,12 @@
 
         return carry
 
-    lax.fori_loop(0, steps + LAG, step, 0)
+    coefficients(jnp.int32(0), jnp.int32(0))
+    load(2).wait()
+    load(3).wait()
+    pl.semaphore_wait(barrier, len(peers) + 4 + NSRC - 1)
+    send_terms(jnp.int32(0), jnp.int32(0))
+    lax.fori_loop(1, steps + LAG, step, 0)
     finish(2 * APPS - 1)
 
     for ph in (2 * APPS - 2, 2 * APPS - 1):
@@ -304,33 +336,34 @@
 def tables(ranks, tile_cols, owner_slot):
     here = lax.axis_index("rows")
     z, m = here // NM, here % NM
-    plane = lax.dynamic_slice_in_dim(tile_cols.reshape(NZ, NM, TILES), z, 1, 0)[0]
+    plane = lax.dynamic_slice_in_dim(tile_cols, z * NM * ROWS_DEV, NM * ROWS_DEV, 0)
     slots = jnp.arange(owner_slot.shape[0], dtype=jnp.int32)
     target = jnp.sum(jnp.where(plane[:, :, None] == slots, owner_slot, 0), axis=2)
     target_dev, local = target // ROWS_DEV, target % ROWS_DEV
-    mine = lax.dynamic_index_in_dim(target_dev, m, 0, keepdims=False)
-    goes = mine[None, :] == jnp.arange(PEERS, dtype=jnp.int32)[:, None]
-    tiles = jnp.arange(TILES, dtype=jnp.int32)
-    values = jnp.stack([tiles, tiles // K, ranks.reshape(TILES)])
-    tab = jnp.sum(jnp.where(goes[None], values[:, None, :], 0), axis=2)
+    mine = lax.dynamic_slice_in_dim(target_dev, m * ROWS_DEV, ROWS_DEV, 0)
+    goes = mine[None] == jnp.arange(PEERS, dtype=jnp.int32)[:, None, None]
+    tile = lax.broadcasted_iota(jnp.int32, (ROWS_DEV, K), 0) * K
+    tile = tile + lax.broadcasted_iota(jnp.int32, (ROWS_DEV, K), 1)
+    tab = jnp.sum(jnp.where(goes, (tile * CODE + ranks)[None], 0), axis=(1, 2))
     layer = jnp.concatenate([z + off for off in offsets_of(jnp.arange(4, dtype=jnp.int32))])
     dest = (layer % NZ) * NM + m
     comes = target_dev[None] == dest[:, None, None]
-    q = jnp.sum(jnp.where(comes, local[None], 0), axis=2).reshape(2, 4, NM)
-    row = jnp.arange(TILES, dtype=jnp.int32)[:, None]
-    col = jnp.arange(NM * SRC, dtype=jnp.int32)[None, :]
-    same = ((row % HALF) == (col % HALF)) & ((row // 32) == (col // HALF % 2))
-    slot = jnp.repeat(q, SRC, axis=2)
-    slot = jnp.where((row // 32)[None] == 0, slot[0][:, None, :], slot[1][:, None, :])
-    onehot = (slot == (row // HALF % ROWS_DEV)[None]) & same[None]
-    return tab.astype(jnp.int32), onehot.astype(BF16)
+    q = jnp.sum(jnp.where(comes, local[None], 0), axis=2)
+    q = jnp.sum(q.reshape(PEERS, ROWS_DEV), axis=1)
+    return tab, q
+
+
+def place_kernel(field_in, grad_in, field_out, grad_out):
+    field_out[...] = field_in[...]
+    grad_out[...] = grad_in[...]
 
 
 def per_device(
     misfit, forward_fields, contrast, u_factors, v_factors, ranks, tile_cols, owner_slot
 ):
-    tab, onehot = tables(ranks, tile_cols, owner_slot)
+    tab, slot_of = tables(ranks, tile_cols, owner_slot)
     vmem = pl.BlockSpec(memory_space=pltpu.VMEM)
+    smem = pl.BlockSpec(memory_space=pltpu.SMEM)
     hbm = pl.BlockSpec(memory_space=pl.ANY)
     dma = pltpu.SemaphoreType.DMA
     field, gradient = pl.pallas_call(
@@ -339,7 +372,7 @@
             jax.ShapeDtypeStruct((TILES, B), F32),
             jax.ShapeDtypeStruct((ROWS_DEV, B), F32),
         ),
-        in_specs=[pl.BlockSpec(memory_space=pltpu.SMEM), vmem, vmem, vmem, vmem, hbm, hbm],
+        in_specs=[smem, vmem, vmem, vmem, smem, hbm, hbm],
         out_specs=(vmem, vmem),
         scratch_shapes=[
             pltpu.VMEM((TILES, RMAX, B), BF16),
@@ -351,8 +384,9 @@
             pltpu.VMEM((2, 4, TILES, B), BF16),
             pltpu.VMEM((4, 4, TILES, B), BF16),
             pltpu.VMEM((2, 32, B), F32),
+            pltpu.VMEM((4, TILES, NM * SRC), BF16),
             pltpu.VMEM((NSRC, ROWS_DEV, B), F32),
-            dma((2,)),
+            dma((4,)),
             dma((2, 4, NM - 1)),
             dma((4, 4, NM)),
             dma((2, 4, 2)),
@@ -368,10 +402,19 @@
         misfit.reshape(TILES, B),
         forward_fields.reshape(TILES, B),
         contrast,
-        onehot,
+        slot_of,
         u_factors.reshape(TILES, RMAX, B),
         v_factors.reshape(TILES, RMAX, B),
     )
+    field, gradient = pl.pallas_call(
+        place_kernel,
+        out_shape=(
+            jax.ShapeDtypeStruct((TILES, B), F32),
+            jax.ShapeDtypeStruct((ROWS_DEV, B), F32),
+        ),
+        in_specs=[vmem, vmem],
+        out_specs=(vmem, vmem),
+    )(field, gradient)
     return field.reshape(ROWS_DEV, SRC, B), gradient
 
 

time: 132 us -> 129 us (0.977)
  local copies, waits for them, and re-layouts: 4.99 us -> 0.93 us
    unnamed x3 -> x2, local copies, waits for them, and re-layouts: 3.81 us -> 0.57 us
    pallas_call x0 -> x1, Pallas kernels: none -> 1.68 us  [per_device(): pl.pallas_call(place_kernel, out_shape=(jax.ShapeDtypeStruct((TILES, B),...]
where the time goes in v3:
time: 129 us
  Pallas kernels  124 us (96%)
  other arithmetic  3.61 us (3%)
    pallas_call x1, Pallas kernels, per_device(): pl.pallas_call(kernel, out_shape=(jax.ShapeDtypeStruct((TILES, B), F32),...  122 us

profile of v3, /device:TPU:1, one launch (start us, length us, event | category | flops | bytes accessed | tf_op | source)
XLA Modules:
  0.0 129.1 jit_solution(14630636446137392044)
XLA Ops:
  0.6 0.0 copy-start
  0.7 0.1 fusion.6
  0.8 0.6 copy-done
  1.4 0.1 constant_dynamic-slice_fusion.1
  1.4 0.1 copy.12
  1.5 1.4 %select_reduce_fusion = s32[32,16]{1,0:T(8,128)S(1)} fusion(s32[256]{0:T(256)} %param.15, s32[32,16]{1,0:T(8,128)S(1)} %copy.12), kind=kLoop, calls=%fused_computation | loop fusion | flops 392704 | bytes 5120 | tf_op jit(solution)/shard_map/reduce_sum | solution.py:341
  2.9 0.1 copy.14
  3.0 0.8 multiply_add_fusion
  3.8 0.1 copy.13
  3.8 0.1 select_reduce_fusion.1
  3.9 0.6 select_reduce_fusion.2.tab
  4.5 0.1 reshape.98
  4.6 0.6 reduce_sum.39.slot_of
  5.2 122.2 %shard_map.95 = (f32[64,1024]{1,0:T(8,128)}, f32[4,1024]{1,0:T(4,128)}) custom-call(s32[64]{0:T(128)} %select_reduce_fusion.2.tab, f32[64,1024]{1,0:T(8,128)} %bitcast.7, bf16[64,1024]{1,0:T(8,128)(2,1)} %bitcast.8, f32[4,1024]{1,0:T(4,128)} %contrast.1, s32[64]{0:T(128)} %reduce_sum.39.slot_of, bf16[64,96,1024]{2,1,0:T(8,128)(2,1)} %bitcast.5, ...), custom_call_target="tpu_custom_call" | custom-call | tf_op jit(solution)/shard_map/pallas_call | solution.py:369
  127.4 1.7 %shard_map.96 = (f32[64,1024]{1,0:T(8,128)}, f32[4,1024]{1,0:T(4,128)}) custom-call(f32[64,1024]{1,0:T(8,128)} %get-tuple-element.6.field_in, f32[4,1024]{1,0:T(4,128)} %get-tuple-element.7.grad_in), custom_call_target="tpu_custom_call" | custom-call | tf_op jit(solution)/shard_map/pallas_call | solution.py:409
  (3 shorter events, 0.0 us)
Async XLA Ops:
  0.6 0.7 copy-start
